TPU v7x, 256 devices: a whole 4x4x8 slice. The times are simulated.
256 devices in a mesh: section: 8 (over x, core), seq: 32 (over z, y).
Axes of the slice: x: 4, y: 4, z: 8, core: 2. Of those that a mesh axis runs over, the one named last changes fastest.
Arguments:
- queries: bfloat16 [8, 10240, 4096], P('section', 'seq'), may hold values from -60 to 60
- keys_new: bfloat16 [8, 10240, 4096], P('section', 'seq'), may hold values from -6 to 6
- values_new: bfloat16 [8, 10240, 4096], P('section', 'seq'), may hold values from -6 to 6
- keys_cache: bfloat16 [8, 6144, 4096], P('section', None, 'seq'), may hold values from -6 to 6
- values_cache: bfloat16 [8, 6144, 4096], P('section', None, 'seq'), may hold values from -6 to 6
- window: int32 [8, 32], P('section', 'seq'), may hold values from 1 to 3, as said below
- global_blocks: int32 [8, 2], P('section'), may hold values from 0 to 95
- random_blocks: int32 [8, 160, 3], P('section'), may hold values from 0 to 95
Outputs:
- handed: bfloat16 [8, 10240, 4096], P('section', 'seq')
Inputs may be any that keep to these rules, and one draw needn't show every extreme that they name: In every section some head has the window 3.
All inputs are finite; a program needn't handle non-finite values.
Results may differ from a plain program's by a relative error of at most 0.0049.
Values may be sent and summed in bfloat16 or wider, within the bound.
A program may use at most 128 MiB of HBM per device.

v0:
```python
import math
import jax
import jax.numpy as jnp
from jax import lax
from jax.sharding import PartitionSpec as P

HD = 128
BLK = 64
WMAX = 3
GLOB = 2
RAND = 3
NK = 8
masked_score = -1e30


def as_sent(shard):

    def short(part):
        return part.astype(jnp.bfloat16) if part.dtype == jnp.float32 else part

    return jax.tree.map(short, shard)


def passed_along(shard, axis, by):
    devices = lax.axis_size(axis)
    return lax.ppermute(shard, axis, [(i, (i + by) % devices) for i in range(devices)])


def block_mask(span_blocks):
    rows = jnp.arange(BLK, dtype=jnp.int32)[:, None]
    column = jnp.arange(NK * BLK, dtype=jnp.int32)[None, :]
    which = column // BLK
    inside = column % BLK
    allowed = jnp.where(which >= WMAX, True, which < span_blocks)
    return allowed & ((which != 0) | (inside <= rows))


def attend_local(
    query,
    fresh_keys,
    fresh_values,
    old_keys,
    old_values,
    span_blocks,
    global_row,
    random_rows,
    group,
):
    stretch_rows = query.shape[0]
    block_count = stretch_rows // BLK
    cache_blocks = old_keys.shape[0] // BLK
    lead = (WMAX - 1) * BLK
    near_keys = jnp.concatenate([old_keys[old_keys.shape[0] - lead :], fresh_keys], axis=0)
    near_values = jnp.concatenate([old_values[old_values.shape[0] - lead :], fresh_values], axis=0)
    glob_keys = jnp.concatenate(
        [lax.dynamic_slice_in_dim(old_keys, global_row[g] * BLK, BLK, 0) for g in range(GLOB)],
        axis=0,
    )
    glob_values = jnp.concatenate(
        [lax.dynamic_slice_in_dim(old_values, global_row[g] * BLK, BLK, 0) for g in range(GLOB)],
        axis=0,
    )
    key_blocks = old_keys.reshape(cache_blocks, BLK, HD)
    value_blocks = old_values.reshape(cache_blocks, BLK, HD)
    query_blocks = query.reshape(block_count, BLK, HD)
    allowed = block_mask(span_blocks)
    scale = 1.0 / math.sqrt(HD)

    def one_group(index):
        first = index * group
        query_part = lax.dynamic_slice_in_dim(query_blocks, first, group, 0)
        near_key_part = lax.dynamic_slice_in_dim(
            near_keys, first * BLK, (group + WMAX - 1) * BLK, 0
        )
        near_value_part = lax.dynamic_slice_in_dim(
            near_values, first * BLK, (group + WMAX - 1) * BLK, 0
        )
        random_part = lax.dynamic_slice_in_dim(random_rows, first, group, 0)
        rand_keys = key_blocks[random_part].reshape(group, RAND * BLK, HD)
        rand_values = value_blocks[random_part].reshape(group, RAND * BLK, HD)
        near_value_list = []
        pieces = []
        for slot in range(WMAX):
            offset = (WMAX - 1 - slot) * BLK
            slot_keys = near_key_part[offset : offset + group * BLK].reshape(group, BLK, HD)
            near_value_list.append(
                near_value_part[offset : offset + group * BLK].reshape(group, BLK, HD)
            )
            pieces.append(
                jnp.einsum(
                    "gih,gjh->gij", query_part, slot_keys, preferred_element_type=jnp.float32
                )
            )
        pieces.append(
            jnp.einsum("gih,jh->gij", query_part, glob_keys, preferred_element_type=jnp.float32)
        )
        pieces.append(
            jnp.einsum("gih,gjh->gij", query_part, rand_keys, preferred_element_type=jnp.float32)
        )
        scores = jnp.concatenate(pieces, axis=2) * scale
        scores = jnp.where(allowed[None], scores, masked_score)
        top = jnp.max(scores, axis=-1, keepdims=True)
        expo = jnp.exp(scores - top)
        weights = (expo / jnp.sum(expo, axis=-1, keepdims=True)).astype(jnp.bfloat16)
        result = jnp.einsum(
            "gij,gjh->gih",
            weights[:, :, WMAX * BLK + GLOB * BLK :],
            rand_values,
            preferred_element_type=jnp.float32,
        )
        result = result + jnp.einsum(
            "gij,jh->gih",
            weights[:, :, WMAX * BLK : WMAX * BLK + GLOB * BLK],
            glob_values,
            preferred_element_type=jnp.float32,
        )
        for slot in range(WMAX):
            result = result + jnp.einsum(
                "gij,gjh->gih",
                weights[:, :, slot * BLK : (slot + 1) * BLK],
                near_value_list[slot],
                preferred_element_type=jnp.float32,
            )
        return result.astype(jnp.bfloat16)

    outputs = lax.map(one_group, jnp.arange(block_count // group, dtype=jnp.int32))
    return outputs.reshape(stretch_rows, HD)


def per_device(
    queries, keys_new, values_new, keys_cache, values_cache, window, global_blocks, random_blocks
):
    head_queries = lax.all_to_all(queries, "seq", split_axis=2, concat_axis=1, tiled=True)
    head_keys, head_values = (
        lax.all_to_all(keys_new, "seq", split_axis=2, concat_axis=1, tiled=True),
        lax.all_to_all(values_new, "seq", split_axis=2, concat_axis=1, tiled=True),
    )
    stretch_rows = head_queries.shape[1]
    block_count = stretch_rows // BLK
    group = math.gcd(block_count, 8)
    global_row = global_blocks[0]
    random_rows = random_blocks[0]
    results = [
        attend_local(
            head_queries[0],
            head_keys[0],
            head_values[0],
            keys_cache[0],
            values_cache[0],
            window[0, 0],
            global_row,
            random_rows,
            group,
        )
    ]
    attended = jnp.concatenate(results, axis=1)[None]
    regrouped = lax.all_to_all(
        as_sent(attended), "seq", split_axis=1, concat_axis=2, tiled=True
    ).astype(attended.dtype)
    return passed_along(as_sent(regrouped), "section", 1).astype(regrouped.dtype)


def solution(mesh):
    placed = (
        P("section", "seq", None),
        P("section", "seq", None),
        P("section", "seq", None),
        P("section", None, "seq"),
        P("section", None, "seq"),
        P("section", "seq"),
        P("section", None),
        P("section", None, None),
    )
    return jax.shard_map(
        per_device, mesh=mesh, in_specs=placed, out_specs=P("section", "seq", None), check_vma=False
    )
```

profile of v0, /device:TPU:32, one launch (start us, length us, event | category | flops | bytes accessed | tf_op | source)
XLA Modules:
  0.0 889.0 jit_solution(13821503862325278436)
XLA Ops:
  0.0 14.3 %copy.46 = bf16[1,320,4096]{1,0,2:T(2,128)(2,1)} copy(bf16[1,320,4096]{2,1,0:T(8,128)(2,1)} %param.12) | data formatting | bytes 5242880 | tf_op args[2]
  14.9 67.0 %reduce.2 = bf16[4096,320]{1,0:T(8,128)(2,1)S(1)} reduce(bf16[4096,1,320]{2,1,0:T(2,128)(2,1)} %bitcast.118, bf16[]{:T(256)} %broadcast.139), dimensions={1}, to_apply=%bitcast.58.reduce_sub_computation | reduce | bytes 5242882
  81.9 4.4 reshape.177
  86.3 12.1 %all-to-all-start.2 = ((bf16[32,2,20480]{2,1,0:T(2,128)(2,1)}), bf16[32,2,20480]{2,1,0:T(2,128)(2,1)}, u32[]{:S(2)}, u32[]{:S(2)}) async-start(bf16[32,2,20480]{2,1,0:T(2,128)(2,1)} %reshape.177), calls=%async_computation.2 | async-start | bytes 5242880 | tf_op jit(solution)/shard_map/all_to_all | solution.py:136
  98.5 12.3 %copy.42 = bf16[1,320,4096]{1,0,2:T(2,128)(2,1)} copy(bf16[1,320,4096]{2,1,0:T(8,128)(2,1)S(1)} %copy-done.2) | data formatting | bytes 5242880 | tf_op args[1]
  110.8 67.0 %reduce.1 = bf16[4096,320]{1,0:T(8,128)(2,1)S(1)} reduce(bf16[4096,1,320]{2,1,0:T(2,128)(2,1)} %bitcast.122, bf16[]{:T(256)} %broadcast.139), dimensions={1}, to_apply=%bitcast.56.reduce_sub_computation | reduce | bytes 5242882
  177.8 4.3 reshape.175
  182.2 10.8 %all-to-all-start.1 = ((bf16[32,2,20480]{2,1,0:T(2,128)(2,1)}), bf16[32,2,20480]{2,1,0:T(2,128)(2,1)}, u32[]{:S(2)}, u32[]{:S(2)}) async-start(bf16[32,2,20480]{2,1,0:T(2,128)(2,1)} %reshape.175), calls=%async_computation.1 | async-start | bytes 5242880 | tf_op jit(solution)/shard_map/all_to_all | solution.py:135
  193.0 12.3 %copy.39 = bf16[1,320,4096]{1,0,2:T(2,128)(2,1)} copy(bf16[1,320,4096]{2,1,0:T(8,128)(2,1)S(1)} %copy-done.3) | data formatting | bytes 5242880 | tf_op args[0]
  205.3 67.0 %reduce = bf16[4096,320]{1,0:T(8,128)(2,1)S(1)} reduce(bf16[4096,1,320]{2,1,0:T(2,128)(2,1)} %bitcast.123, bf16[]{:T(256)} %broadcast.139), dimensions={1}, to_apply=%bitcast.54.reduce_sub_computation | reduce | bytes 5242882
  272.4 4.4 reshape.173
  276.8 10.3 %all-to-all-start = ((bf16[32,2,20480]{2,1,0:T(2,128)(2,1)}), bf16[32,2,20480]{2,1,0:T(2,128)(2,1)}, u32[]{:S(2)}, u32[]{:S(2)}) async-start(bf16[32,2,20480]{2,1,0:T(2,128)(2,1)} %reshape.173), calls=%async_computation | async-start | bytes 5242880 | tf_op jit(solution)/shard_map/all_to_all | solution.py:133
  292.1 19.9 %reshape.178 = bf16[4096,1,320]{2,1,0:T(2,128)(2,1)} reshape(bf16[32,2,20480]{2,1,0:T(2,128)(2,1)} %all-to-all-done.2) | data formatting | bytes 5242880
  318.6 4.2 copy.48
  322.8 19.9 %reshape.176 = bf16[4096,1,320]{2,1,0:T(2,128)(2,1)} reshape(bf16[32,2,20480]{2,1,0:T(2,128)(2,1)} %all-to-all-done.1) | data formatting | bytes 5242880
  349.2 4.3 copy.44
  353.6 19.9 %reshape.174 = bf16[4096,1,320]{2,1,0:T(2,128)(2,1)} reshape(bf16[32,2,20480]{2,1,0:T(2,128)(2,1)} %all-to-all-done) | data formatting | bytes 5242880
  380.1 4.4 copy.41
  387.1 322.0 %while.13 = (s32[]{:T(128)}, bf16[20,8,64,128]{3,2,1,0:T(8,128)(2,1)}, s32[20]{0:T(128)S(1)}, bf16[160,64,128]{2,1,0:T(8,128)(2,1)}, bf16[10368,128]{1,0:T(8,128...) while((s32[]{:T(128)}, ...), condition=%wide.region_3.4_spmd.clone, body=%wide.region_0.3_spmd.clone.sunk | while | flops 136218192 | bytes 15348233 | solution.py:126
  709.1 6.0 copy.62
  715.0 56.2 %reduce.3 = bf16[10240,128]{1,0:T(8,128)(2,1)S(1)} reduce(bf16[10240,1,128]{2,1,0:T(2,128)(2,1)} %bitcast.124, bf16[]{:T(256)} %broadcast.139), dimensions={1}, to_apply=%bitcast.72.reduce_sub_computation | reduce | bytes 5242882
  773.5 70.3 %all_to_all.63 = bf16[32,2,20480]{2,1,0:T(2,128)(2,1)S(1)} all-to-all(bf16[32,2,20480]{2,1,0:T(2,128)(2,1)} %reshape.179), channel_id=1, replica_groups=mesh['section'=8,'seq'=32] {'seq'}, dimensions={0} | all-to-all | bytes 5242880 | tf_op jit(solution)/shard_map/all_to_all | solution.py:157
  843.8 7.2 reshape.180
  855.0 32.3 %collective-permute-done = bf16[1,320,4096]{2,1,0:T(8,128)(2,1)S(1)} collective-permute-done((bf16[1,320,4096]{2,1,0:T(8,128)(2,1)S(1)}, bf16[1,320,4096]{2,1,0:T(8,128)(2,1)S(1)}, u32[]{:S(2)}, u32[]{:S(2)}) %collective-permute-start) | collective-permute-done | bytes 2621472 | tf_op jit(solution)/shard_map/ppermute | solution.py:26
  (459 shorter events, 327.9 us)
Async XLA Ops:
  86.3 12.2 %copy-start.2 = (bf16[1,320,4096]{2,1,0:T(8,128)(2,1)S(1)}, bf16[1,320,4096]{2,1,0:T(8,128)(2,1)}, u32[]{:S(2)}) copy-start(bf16[1,320,4096]{2,1,0:T(8,128)(2,1)} %param.11) | copy-start | bytes 7864324
  86.3 95.9 %all-to-all-start.2 = ((bf16[32,2,20480]{2,1,0:T(2,128)(2,1)}), bf16[32,2,20480]{2,1,0:T(2,128)(2,1)}, u32[]{:S(2)}, u32[]{:S(2)}) async-start(bf16[32,2,20480]{2,1,0:T(2,128)(2,1)} %reshape.177), calls=%async_computation.2 | async-start | bytes 5242880 | tf_op jit(solution)/shard_map/all_to_all | solution.py:136
  182.2 10.8 %copy-start.3 = (bf16[1,320,4096]{2,1,0:T(8,128)(2,1)S(1)}, bf16[1,320,4096]{2,1,0:T(8,128)(2,1)}, u32[]{:S(2)}) copy-start(bf16[1,320,4096]{2,1,0:T(8,128)(2,1)} %param.10) | copy-start | bytes 7864324
  182.2 94.6 %all-to-all-start.1 = ((bf16[32,2,20480]{2,1,0:T(2,128)(2,1)}), bf16[32,2,20480]{2,1,0:T(2,128)(2,1)}, u32[]{:S(2)}, u32[]{:S(2)}) async-start(bf16[32,2,20480]{2,1,0:T(2,128)(2,1)} %reshape.175), calls=%async_computation.1 | async-start | bytes 5242880 | tf_op jit(solution)/shard_map/all_to_all | solution.py:135
  276.8 10.3 %copy-start.5 = (s32[1,2]{1,0:T(1,128)S(1)}, s32[1,2]{1,0:T(1,128)}, u32[]{:S(2)}) copy-start(s32[1,2]{1,0:T(1,128)} %param.16) | copy-start | bytes 28
  276.8 12.9 %copy-start.4 = (s32[1,160,3]{1,0,2:T(1,128)S(1)}, s32[1,160,3]{1,0,2:T(1,128)}, u32[]{:S(2)}) copy-start(s32[1,160,3]{1,0,2:T(1,128)} %param.17) | copy-start | bytes 5764
  276.8 76.8 %all-to-all-start = ((bf16[32,2,20480]{2,1,0:T(2,128)(2,1)}), bf16[32,2,20480]{2,1,0:T(2,128)(2,1)}, u32[]{:S(2)}, u32[]{:S(2)}) async-start(bf16[32,2,20480]{2,1,0:T(2,128)(2,1)} %reshape.173), calls=%async_computation | async-start | bytes 5242880 | tf_op jit(solution)/shard_map/all_to_all | solution.py:133
  380.1 4.4 copy-start
  380.1 4.4 copy-start.1
  855.0 32.3 %collective-permute-start = (bf16[1,320,4096]{2,1,0:T(8,128)(2,1)S(1)}, bf16[1,320,4096]{2,1,0:T(8,128)(2,1)S(1)}, u32[]{:S(2)}, u32[]{:S(2)}) collective-permute-start(bf16[1,320,4096]{2,1,0:T(8,128)(2,1)S(1)} %bitcast.143), channel_id=1, source_target_pairs={{0,32},{32,64},{64,96},{96,128},{128,160},{160,192},{192,224},{224... | collective-permute-start | bytes 7864328 | tf_op jit(solution)/shard_map/ppermute | solution.py:26
where the time goes:
time: 903 us; the launch traced here: 889 us
  local copies, waits for them, and re-layouts  304 us (34%)
  other arithmetic  271 us (30%)
  matrix products  148 us (16%)
  blocking collectives  70.3 us (8%)
  starting transfers between devices  33.3 us (4%)
  waiting for transfers between devices  32.3 us (4%)
  loops' own time  27.7 us (3%)
    unnamed x4, other arithmetic  257 us
    unnamed x30, local copies, waits for them, and re-layouts  137 us
    all_to_all x1, blocking collectives, per_device(): lax.all_to_all(as_sent(attended), 'seq', split_axis=1, concat_axis=2, til...  70.3 us
    dot_general x60, matrix products, one_group(): jnp.einsum('gih,gjh->gij', query_part, slot_keys, preferred_element_type=...  65.6 us
    gather x20, local copies, waits for them, and re-layouts, one_group(): rand_values = value_blocks[random_part].reshape(group, RAND * BLK, HD)  40.6 us
    gather x20, local copies, waits for them, and re-layouts, one_group(): rand_keys = key_blocks[random_part].reshape(group, RAND * BLK, HD)  40.6 us
    ppermute x1, waiting for transfers between devices, passed_along(): lax.ppermute(shard, axis, [(i, (i + by) % devices) for i in range(devices)])  32.3 us
    another operation x1, loops' own time, attend_local(): lax.map(one_group, jnp.arange(block_count // group, dtype=jnp.int32))  27.7 us
  transfers between devices with their start and end apart: 4, of which 1 were waited for; matrix products, arithmetic and copies ran while one was open for 26% of the time, Pallas kernels for 0%

commit v1 on v0

--- a/solution.py
+++ b/solution.py
@@ -154,8 +154,11 @@
         )
     ]
     attended = jnp.concatenate(results, axis=1)[None]
-    regrouped = lax.all_to_all(
-        as_sent(attended), "seq", split_axis=1, concat_axis=2, tiled=True
+    regrouped = jnp.concatenate(
+        lax.all_to_all(
+            jnp.stack(jnp.split(as_sent(attended), lax.axis_size("seq"), axis=1)), "seq", 0, 0
+        ),
+        axis=2,
     ).astype(attended.dtype)
     return passed_along(as_sent(regrouped), "section", 1).astype(regrouped.dtype)
 

time: 903 us -> 850 us (0.941)
  other arithmetic: 271 us -> 215 us
    unnamed x4 -> x3, other arithmetic: 257 us -> 201 us
    unnamed x30 -> x58, local copies, waits for them, and re-layouts: 137 us -> 152 us
  transfers between devices with their start and end apart: 4 -> 4, of which waited for: 1 -> 1; matrix products, arithmetic and copies ran while one was open for 26% -> 28% of each run, Pallas kernels for 0% -> 0%
where the time goes in v1:
time: 850 us; the launch traced here: 840 us
  local copies, waits for them, and re-layouts  312 us (37%)
  other arithmetic  215 us (25%)
  matrix products  148 us (17%)
  blocking collectives  70.1 us (8%)
  waiting for transfers between devices  32.3 us (4%)
  starting transfers between devices  31.8 us (4%)
  loops' own time  28.3 us (3%)
    unnamed x3, other arithmetic  201 us
    unnamed x58, local copies, waits for them, and re-layouts  152 us
    all_to_all x1, blocking collectives, per_device(): lax.all_to_all(jnp.stack(jnp.split(as_sent(attended), lax.axis_size('seq'...  70.1 us
    dot_general x60, matrix products, one_group(): jnp.einsum('gih,gjh->gij', query_part, slot_keys, preferred_element_type=...  65.6 us
    gather x20, local copies, waits for them, and re-layouts, one_group(): rand_keys = key_blocks[random_part].reshape(group, RAND * BLK, HD)  40.6 us
    gather x20, local copies, waits for them, and re-layouts, one_group(): rand_values = value_blocks[random_part].reshape(group, RAND * BLK, HD)  40.6 us
    ppermute x1, waiting for transfers between devices, passed_along(): lax.ppermute(shard, axis, [(i, (i + by) % devices) for i in range(devices)])  32.3 us
    another operation x1, loops' own time, attend_local(): lax.map(one_group, jnp.arange(block_count // group, dtype=jnp.int32))  28.3 us
  transfers between devices with their start and end apart: 4, of which 1 were waited for; matrix products, arithmetic and copies ran while one was open for 28% of the time, Pallas kernels for 0%

profile of v1, /device:TPU:32, one launch (start us, length us, event | category | flops | bytes accessed | tf_op | source)
XLA Modules:
  0.0 840.0 jit_solution(10011276780195649076)
XLA Ops:
  0.0 14.3 %copy.76 = bf16[1,320,4096]{1,0,2:T(2,128)(2,1)} copy(bf16[1,320,4096]{2,1,0:T(8,128)(2,1)} %param.12) | data formatting | bytes 5242880 | tf_op args[2]
  14.8 67.0 %reduce.2 = bf16[4096,320]{1,0:T(8,128)(2,1)S(1)} reduce(bf16[4096,1,320]{2,1,0:T(2,128)(2,1)} %bitcast.241, bf16[]{:T(256)} %broadcast.139), dimensions={1}, to_apply=%bitcast.184.reduce_sub_computation | reduce | bytes 5242882
  81.8 4.4 reshape.185
  86.2 11.7 %all-to-all-start.2 = ((bf16[32,2,20480]{2,1,0:T(2,128)(2,1)}), bf16[32,2,20480]{2,1,0:T(2,128)(2,1)}, u32[]{:S(2)}, u32[]{:S(2)}) async-start(bf16[32,2,20480]{2,1,0:T(2,128)(2,1)} %reshape.185), calls=%async_computation.2 | async-start | bytes 5242880 | tf_op jit(solution)/shard_map/all_to_all | solution.py:136
  97.9 12.3 %copy.72 = bf16[1,320,4096]{1,0,2:T(2,128)(2,1)} copy(bf16[1,320,4096]{2,1,0:T(8,128)(2,1)S(1)} %copy-done.2) | data formatting | bytes 5242880 | tf_op args[1]
  110.2 67.0 %reduce.1 = bf16[4096,320]{1,0:T(8,128)(2,1)S(1)} reduce(bf16[4096,1,320]{2,1,0:T(2,128)(2,1)} %bitcast.246, bf16[]{:T(256)} %broadcast.139), dimensions={1}, to_apply=%bitcast.182.reduce_sub_computation | reduce | bytes 5242882
  177.2 4.3 reshape.183
  181.5 10.1 %all-to-all-start.1 = ((bf16[32,2,20480]{2,1,0:T(2,128)(2,1)}), bf16[32,2,20480]{2,1,0:T(2,128)(2,1)}, u32[]{:S(2)}, u32[]{:S(2)}) async-start(bf16[32,2,20480]{2,1,0:T(2,128)(2,1)} %reshape.183), calls=%async_computation.1 | async-start | bytes 5242880 | tf_op jit(solution)/shard_map/all_to_all | solution.py:135
  191.6 12.3 %copy.69 = bf16[1,320,4096]{1,0,2:T(2,128)(2,1)} copy(bf16[1,320,4096]{2,1,0:T(8,128)(2,1)S(1)} %copy-done.3) | data formatting | bytes 5242880 | tf_op args[0]
  204.0 67.0 %reduce = bf16[4096,320]{1,0:T(8,128)(2,1)S(1)} reduce(bf16[4096,1,320]{2,1,0:T(2,128)(2,1)} %bitcast.242, bf16[]{:T(256)} %broadcast.139), dimensions={1}, to_apply=%bitcast.180.reduce_sub_computation | reduce | bytes 5242882
  270.9 4.4 reshape.181
  275.3 10.0 %all-to-all-start = ((bf16[32,2,20480]{2,1,0:T(2,128)(2,1)}), bf16[32,2,20480]{2,1,0:T(2,128)(2,1)}, u32[]{:S(2)}, u32[]{:S(2)}) async-start(bf16[32,2,20480]{2,1,0:T(2,128)(2,1)} %reshape.181), calls=%async_computation | async-start | bytes 5242880 | tf_op jit(solution)/shard_map/all_to_all | solution.py:133
  290.2 19.8 %reshape.186 = bf16[4096,1,320]{2,1,0:T(2,128)(2,1)} reshape(bf16[32,2,20480]{2,1,0:T(2,128)(2,1)} %all-to-all-done.2) | data formatting | bytes 5242880
  310.0 3.3 copy.85
  316.6 4.2 copy.78
  320.8 19.8 %reshape.184 = bf16[4096,1,320]{2,1,0:T(2,128)(2,1)} reshape(bf16[32,2,20480]{2,1,0:T(2,128)(2,1)} %all-to-all-done.1) | data formatting | bytes 5242880
  340.6 3.3 copy.84
  347.2 4.3 copy.74
  351.5 19.8 %reshape.182 = bf16[4096,1,320]{2,1,0:T(2,128)(2,1)} reshape(bf16[32,2,20480]{2,1,0:T(2,128)(2,1)} %all-to-all-done) | data formatting | bytes 5242880
  371.3 3.3 copy.83
  377.9 4.4 copy.71
  384.9 321.9 %while.13 = (s32[]{:T(128)}, bf16[20,8,64,128]{3,2,1,0:T(8,128)(2,1)}, s32[20]{0:T(128)S(1)}, bf16[160,64,128]{2,1,0:T(8,128)(2,1)}, bf16[10368,128]{1,0:T(8,128...) while((s32[]{:T(128)}, ...), condition=%wide.region_3.4_spmd.clone, body=%wide.region_0.3_spmd.clone.sunk | while | flops 136218192 | bytes 15348233 | solution.py:126
  735.7 70.1 %all_to_all.50 = bf16[32,1,320,128]{3,2,1,0:T(8,128)(2,1)S(1)} all-to-all(bf16[32,1,320,128]{3,2,1,0:T(8,128)(2,1)S(1)} %fusion.39), channel_id=1, replica_groups=mesh['section'=8,'seq'=32] {'seq'}, dimensions={0} | all-to-all | bytes 5242880 | tf_op jit(solution)/shard_map/all_to_all | solution.py:158
  806.3 32.3 %collective-permute-done = bf16[1,320,4096]{2,1,0:T(8,128)(2,1)S(1)} collective-permute-done((bf16[1,320,4096]{2,1,0:T(8,128)(2,1)S(1)}, bf16[1,320,4096]{2,1,0:T(8,128)(2,1)S(1)}, u32[]{:S(2)}, u32[]{:S(2)}) %collective-permute-start) | collective-permute-done | bytes 2621472 | tf_op jit(solution)/shard_map/ppermute | solution.py:26
  (486 shorter events, 340.2 us)
Async XLA Ops:
  86.2 11.7 %copy-start.2 = (bf16[1,320,4096]{2,1,0:T(8,128)(2,1)S(1)}, bf16[1,320,4096]{2,1,0:T(8,128)(2,1)}, u32[]{:S(2)}) copy-start(bf16[1,320,4096]{2,1,0:T(8,128)(2,1)} %param.11) | copy-start | bytes 7864324
  86.2 95.3 %all-to-all-start.2 = ((bf16[32,2,20480]{2,1,0:T(2,128)(2,1)}), bf16[32,2,20480]{2,1,0:T(2,128)(2,1)}, u32[]{:S(2)}, u32[]{:S(2)}) async-start(bf16[32,2,20480]{2,1,0:T(2,128)(2,1)} %reshape.185), calls=%async_computation.2 | async-start | bytes 5242880 | tf_op jit(solution)/shard_map/all_to_all | solution.py:136
  181.5 10.1 %copy-start.3 = (bf16[1,320,4096]{2,1,0:T(8,128)(2,1)S(1)}, bf16[1,320,4096]{2,1,0:T(8,128)(2,1)}, u32[]{:S(2)}) copy-start(bf16[1,320,4096]{2,1,0:T(8,128)(2,1)} %param.10) | copy-start | bytes 7864324
  181.5 93.8 %all-to-all-start.1 = ((bf16[32,2,20480]{2,1,0:T(2,128)(2,1)}), bf16[32,2,20480]{2,1,0:T(2,128)(2,1)}, u32[]{:S(2)}, u32[]{:S(2)}) async-start(bf16[32,2,20480]{2,1,0:T(2,128)(2,1)} %reshape.183), calls=%async_computation.1 | async-start | bytes 5242880 | tf_op jit(solution)/shard_map/all_to_all | solution.py:135
  275.3 10.0 %copy-start.5 = (s32[1,2]{1,0:T(1,128)S(1)}, s32[1,2]{1,0:T(1,128)}, u32[]{:S(2)}) copy-start(s32[1,2]{1,0:T(1,128)} %param.16) | copy-start | bytes 28
  275.3 12.4 %copy-start.4 = (s32[1,160,3]{1,0,2:T(1,128)S(1)}, s32[1,160,3]{1,0,2:T(1,128)}, u32[]{:S(2)}) copy-start(s32[1,160,3]{1,0,2:T(1,128)} %param.17) | copy-start | bytes 5764
  275.3 76.2 %all-to-all-start = ((bf16[32,2,20480]{2,1,0:T(2,128)(2,1)}), bf16[32,2,20480]{2,1,0:T(2,128)(2,1)}, u32[]{:S(2)}, u32[]{:S(2)}) async-start(bf16[32,2,20480]{2,1,0:T(2,128)(2,1)} %reshape.181), calls=%async_computation | async-start | bytes 5242880 | tf_op jit(solution)/shard_map/all_to_all | solution.py:133
  377.9 4.4 copy-start
  377.9 4.4 copy-start.1
  806.2 32.3 %collective-permute-start = (bf16[1,320,4096]{2,1,0:T(8,128)(2,1)S(1)}, bf16[1,320,4096]{2,1,0:T(8,128)(2,1)S(1)}, u32[]{:S(2)}, u32[]{:S(2)}) collective-permute-start(bf16[1,320,4096]{2,1,0:T(8,128)(2,1)S(1)} %copy_bitcast_fusion), channel_id=1, source_target_pairs={{0,32},{32,64},{64,96},{96,128},{128,160},{160,192},{192,224},{224... | collective-permute-start | bytes 7864328 | tf_op jit(solution)/shard_map/ppermute | solution.py:26
